TPU v7x, 128 devices: a whole 4x4x4 slice. The times are simulated.
128 devices in a mesh: row: 8 (over y, x_lo), col: 16 (over z, x_hi, core).
Axes of the slice: x: 4 (x_hi: 2, x_lo: 2; x = x_hi * 2 + x_lo), y: 4, z: 4, core: 2. Of those that a mesh axis runs over, the one named last changes fastest.
Arguments:
- pair: bfloat16 [256, 256, 128], P('row', 'col'), may hold values from -6 to 6
- cotangent: bfloat16 [256, 256, 128], P('row', 'col'), may hold values from -6 to 6
- token_mask: int32 [256], replicated, may hold values 0 or 1
- out_in_proj: bfloat16 [128, 640], replicated, may hold values from -0.5 to 0.5
- out_out_proj: bfloat16 [128, 128], replicated, may hold values from -0.5 to 0.5
- in_in_proj: bfloat16 [128, 640], replicated, may hold values from -0.5 to 0.5
- in_out_proj: bfloat16 [128, 128], replicated, may hold values from -0.5 to 0.5
Outputs:
- updated_pair: bfloat16 [256, 256, 128], P('row', 'col')
- pair_grad: bfloat16 [256, 256, 128], P('row', 'col')
- out_in_grad: float32 [128, 640], replicated
- out_out_grad: float32 [128, 128], replicated
- in_in_grad: float32 [128, 640], replicated
- in_out_grad: float32 [128, 128], replicated
All inputs are finite; a program needn't handle non-finite values.
Results may differ from a plain program's by a relative error of at most 0.012.
Values may be sent and summed in bfloat16 or wider, within the bound.
A program may use at most 128 MiB of HBM per device.

v0:
```python
import jax
import jax.numpy as jnp
from jax import lax
from jax.sharding import PartitionSpec as P

H = 128
EPSILON = 1e-05


def shortened(array):
    return jax.tree.map(lambda a: a.astype(jnp.bfloat16) if a.dtype == jnp.float32 else a, array)


def from_everyone(array, axis):
    copies = jnp.broadcast_to(array, (lax.axis_size(axis), *array.shape))
    return lax.all_to_all(copies, axis, split_axis=0, concat_axis=0, tiled=True)


def in_order(tiles, dim):
    shape = list(tiles.shape[1:])
    shape[dim] *= tiles.shape[0]
    return jnp.moveaxis(tiles, 0, dim).reshape(shape)


def collect(array, axis, dim):
    tiles = from_everyone(array, axis)
    return in_order(tiles, dim)


def normalize(values):
    centre = jnp.mean(values, axis=-1, keepdims=True)
    shifted = values - centre
    spread = jnp.mean(shifted * shifted, axis=-1, keepdims=True)
    return shifted * lax.rsqrt(spread + EPSILON)


def gating(projected, pair_mask):
    left_value = projected[..., :H]
    left_gate = projected[..., H : 2 * H]
    right_value = projected[..., 2 * H : 3 * H]
    right_gate = projected[..., 3 * H : 4 * H]
    left_full = jax.nn.sigmoid(left_gate) * left_value * pair_mask
    right_full = jax.nn.sigmoid(right_gate) * right_value * pair_mask
    return (left_full, right_full, jax.nn.sigmoid(projected[..., 4 * H :]))


def cols_of(tiles):
    return jax.tree.map(
        lambda part, own: part.astype(own.dtype),
        lax.all_gather(shortened(tiles), "col", axis=1, tiled=True),
        tiles,
    )


def rows_of(tiles):
    return jax.tree.map(
        lambda part, own: part.astype(own.dtype),
        jax.tree.map(lambda part: collect(part, "row", 0), shortened(tiles)),
        tiles,
    )


def to_row_blocks(panel):
    return lax.all_to_all(panel, "col", split_axis=0, concat_axis=1, tiled=True)


def to_col_blocks(panel):
    return lax.all_to_all(panel, "row", split_axis=1, concat_axis=0, tiled=True)


def outgoing_sum(left_tile, right_tile):
    row_panels = rows_of((left_tile, right_tile))
    left_panel = cols_of(left_tile)
    right_rows = to_row_blocks(row_panels[1])
    total = jnp.einsum("ikh,jkh->ijh", left_panel, right_rows, preferred_element_type=jnp.float32)
    return (total, row_panels)


def incoming_sum(left_tile, right_tile):
    col_panels = cols_of((left_tile, right_tile))
    right_all = rows_of(right_tile)
    left_cols = to_col_blocks(col_panels[0])
    total = jnp.einsum("kih,kjh->ijh", left_cols, right_all, preferred_element_type=jnp.float32)
    return (total, col_panels)


def outgoing_grads(tri_grad, row_panels):
    grad_cols = cols_of(tri_grad)
    grad_rows = to_col_blocks(grad_cols)
    left_grad = jnp.einsum(
        "ijh,jkh->ikh", grad_cols, row_panels[1], preferred_element_type=jnp.float32
    )
    right_grad = jnp.einsum(
        "ijh,ikh->jkh", grad_rows, row_panels[0], preferred_element_type=jnp.float32
    )
    return (left_grad, right_grad)


def incoming_grads(tri_grad, col_panels):
    grad_rows = rows_of(tri_grad)
    grad_cols = to_row_blocks(grad_rows)
    left_grad = jnp.einsum(
        "ijh,kjh->kih", grad_cols, col_panels[1], preferred_element_type=jnp.float32
    )
    right_grad = jnp.einsum(
        "kih,ijh->kjh", col_panels[0], grad_rows, preferred_element_type=jnp.float32
    )
    return (left_grad, right_grad)


def forward(pair_in, pair_mask, w_in, w_out, outgoing):
    pair_wide = pair_in.astype(jnp.float32)
    normed = normalize(pair_wide).astype(jnp.bfloat16)
    projected = jnp.dot(normed, w_in, preferred_element_type=jnp.float32)
    left_full, right_full, gate = gating(projected, pair_mask)
    left_tile = left_full.astype(jnp.bfloat16)
    right_tile = right_full.astype(jnp.bfloat16)
    if outgoing:
        triangle_sum, panels = outgoing_sum(left_tile, right_tile)
    else:
        triangle_sum, panels = incoming_sum(left_tile, right_tile)
    tri_normed = normalize(triangle_sum).astype(jnp.bfloat16)
    lifted = jnp.dot(tri_normed, w_out, preferred_element_type=jnp.float32)
    result = (pair_wide + gate * lifted).astype(jnp.bfloat16)
    saved = (pair_wide, normed, projected, gate, triangle_sum, tri_normed, lifted, panels)
    return (result, saved)


def backward(cotan, saved, pair_mask, w_in, w_out, outgoing):
    pair_wide, normed, projected, gate, triangle_sum, tri_normed, lifted, panels = saved
    cot_wide = cotan.astype(jnp.float32)
    lift_grad = gate * cot_wide
    gate_grad = lifted * cot_wide
    out_grad = jnp.einsum(
        "ijh,ijc->hc", tri_normed.astype(jnp.float32), lift_grad, precision=lax.Precision.HIGHEST
    )
    normed_tri_grad = jnp.dot(
        lift_grad, w_out.astype(jnp.float32).T, precision=lax.Precision.HIGHEST
    )
    tri_grad = jax.vjp(normalize, triangle_sum)[1](normed_tri_grad)[0].astype(jnp.bfloat16)
    if outgoing:
        left_grad, right_grad = outgoing_grads(tri_grad, panels)
    else:
        left_grad, right_grad = incoming_grads(tri_grad, panels)
    gate_vjp = jax.vjp(lambda values: gating(values, pair_mask), projected)[1]
    proj_grad = gate_vjp((left_grad, right_grad, gate_grad))[0]
    in_grad = jnp.einsum(
        "ijc,ijq->cq", normed.astype(jnp.float32), proj_grad, precision=lax.Precision.HIGHEST
    )
    normed_grad = jnp.dot(proj_grad, w_in.astype(jnp.float32).T, precision=lax.Precision.HIGHEST)
    pair_grad = (cot_wide + jax.vjp(normalize, pair_wide)[1](normed_grad)[0]).astype(jnp.bfloat16)
    return (pair_grad, in_grad, out_grad)


def local(pair, cotangent, token_mask, out_in_proj, out_out_proj, in_in_proj, in_out_proj):
    row_tile = pair.shape[0]
    col_tile = pair.shape[1]
    row_flags = lax.dynamic_slice_in_dim(
        token_mask, lax.axis_index("row") * row_tile, row_tile, 0
    ).astype(jnp.float32)
    col_flags = lax.dynamic_slice_in_dim(
        token_mask, lax.axis_index("col") * col_tile, col_tile, 0
    ).astype(jnp.float32)
    pair_mask = (row_flags[:, None] * col_flags[None, :])[:, :, None]
    middle, saved_out = forward(pair, pair_mask, out_in_proj, out_out_proj, True)
    updated, saved_in = forward(middle, pair_mask, in_in_proj, in_out_proj, False)
    middle_grad, in_in_part, in_out_part = backward(
        cotangent, saved_in, pair_mask, in_in_proj, in_out_proj, False
    )
    pair_grad, out_in_part, out_out_part = backward(
        middle_grad, saved_out, pair_mask, out_in_proj, out_out_proj, True
    )
    totals = lax.psum((out_in_part, out_out_part, in_in_part, in_out_part), ("row", "col"))
    tokens_all = row_tile * lax.axis_size("row")
    return (
        updated,
        pair_grad,
        totals[0] / tokens_all,
        totals[1] / tokens_all,
        totals[2] / tokens_all,
        totals[3] / tokens_all,
    )


def solution(mesh):
    return jax.shard_map(
        local,
        mesh=mesh,
        in_specs=(P("row", "col", None), P("row", "col", None), P(), P(), P(), P(), P()),
        out_specs=(P("row", "col", None), P("row", "col", None), P(), P(), P(), P()),
        check_vma=False,
    )
```

profile of v0, /device:TPU:1, one launch (start us, length us, event | category | flops | bytes accessed | tf_op | source)
XLA Modules:
  0.0 564.3 jit_solution(1086619950908574980)
XLA Ops:
  14.3 22.1 %all_to_all.92 = bf16[8,32,16,128]{3,2,1,0:T(8,128)(2,1)S(1)} all-to-all(bf16[8,32,16,128]{3,2,1,0:T(8,128)(2,1)S(1)} %broadcast_in_dim.24), channel_id=1, replica_groups=mesh['row'=8,'col'=16] {'row'}, dimensions={0} | all-to-all | bytes 2097152 | tf_op jit(solution)/shard_map/all_to_all | solution.py:16
  36.4 31.5 %all_to_all.93 = bf16[256,16,128]{2,1,0:T(8,128)(2,1)S(1)} all-to-all(bf16[256,16,128]{2,1,0:T(8,128)(2,1)S(1)} %bitcast.135), channel_id=1, replica_groups=mesh['row'=8,'col'=16] {'col'}, dimensions={0} | all-to-all | bytes 2097152 | tf_op jit(solution)/shard_map/all_to_all | solution.py:64
  69.1 2.7 copy.220
  72.3 15.3 %copy.221 = bf16[32,256,128]{0,1,2:T(8,128)(2,1)} copy(bf16[32,256,128]{2,1,0:T(8,128)(2,1)} %all-gather.5.cloned.1.call-done) | data formatting | bytes 4194304 | tf_op jit(solution)/shard_map/all_gather | solution.py:50
  87.6 6.0 %bitcast_reduce_fusion.1 = (f32[32,16]{0,1:T(8,128)S(1)}, f32[128,16,32]{2,1,0:T(8,128)}) fusion(bf16[16,256,128]{1,0,2:T(8,128)(2,1)} %copy.220, bf16[32,256,128]{0,1,2:T(8,128)(2,1)} %copy.221), kind=kOutput, calls=%fused_computation.7 | convolution fusion | flops 33619456 | bytes 3409920 | tf_op jit(solution)/shard_map/ikh,jkh->ijh/dot_general | solution.py:75
  93.6 1.7 copy.222
  101.4 4.2 all-to-all-start.2
  105.7 40.1 %all-gather.7.cloned.1.call-done = bf16[32,256,128]{2,1,0:T(8,128)(2,1)} async-done(((bf16[32,16,128]{2,1,0:T(8,128)(2,1)}), bf16[32,256,128]{2,1,0:T(8,128)(2,1)}) %all-gather.7.cloned.1.call-update) | async-done | bytes 2097168 | tf_op jit(solution)/shard_map/all_gather | solution.py:50
  145.8 4.3 copy.231
  150.1 4.4 all-to-all-start.3
  155.2 3.0 copy.234
  158.2 24.5 %all-to-all-done.3 = bf16[32,256,128]{2,0,1:T(8,128)(2,1)} async-done(((bf16[32,256,128]{2,0,1:T(8,128)(2,1)}), bf16[32,256,128]{2,0,1:T(8,128)(2,1)}, u32[]{:S(2)}, u32[]{:S(2)}) %all-to-all-start.3) | async-done | bytes 2097184 | tf_op jit(solution)/shard_map/all_to_all | solution.py:68
  182.6 3.7 copy.233
  186.4 4.9 copy.235
  191.3 3.6 bitcast_reduce_fusion
  194.8 1.7 copy.236
  196.6 2.0 multiply_reduce_fusion.1
  201.9 17.9 %all_to_all.94 = bf16[8,32,16,128]{3,2,1,0:T(8,128)(2,1)} all-to-all(bf16[8,32,16,128]{3,2,1,0:T(8,128)(2,1)S(1)} %broadcast_in_dim.28), channel_id=1, replica_groups=mesh['row'=8,'col'=16] {'row'}, dimensions={0} | all-to-all | bytes 2097152 | tf_op jit(solution)/shard_map/all_to_all | solution.py:16
  219.8 6.1 %all-to-all-start.5 = ((bf16[256,16,128]{2,1,0:T(8,128)(2,1)}), bf16[256,16,128]{2,1,0:T(8,128)(2,1)}, u32[]{:S(2)}, u32[]{:S(2)}) async-start(bf16[256,16,128]{2,1,0:T(8,128)(2,1)} %bitcast.137), calls=%async_computation.5 | async-start | bytes 2097152 | tf_op jit(solution)/shard_map/all_to_all | solution.py:64
  225.9 15.2 %copy.246 = bf16[32,256,128]{0,1,2:T(8,128)(2,1)} copy(bf16[32,256,128]{2,1,0:T(8,128)(2,1)} %all-gather.7.cloned.1.call-done) | data formatting | bytes 4194304 | tf_op jit(solution)/shard_map/all_gather | solution.py:50
  241.2 15.3 %copy.249 = bf16[32,256,128]{0,1,2:T(8,128)(2,1)} copy(bf16[32,256,128]{2,1,0:T(8,128)(2,1)} %all-gather.9.cloned.1.call-done) | data formatting | bytes 4194304 | tf_op jit(solution)/shard_map/all_gather | solution.py:50
  256.5 3.0 copy.245
  259.4 5.9 %fusion.83 = f32[128,16,32]{2,1,0:T(8,128)} fusion(bf16[256,16,128]{0,1,2:T(8,128)(2,1)} %copy.245, bf16[32,256,128]{0,1,2:T(8,128)(2,1)} %copy.246), kind=kOutput, calls=%fused_computation.151 | convolution fusion | flops 33554432 | bytes 3407872 | tf_op jit(solution)/shard_map/kih,ijh->kjh/dot_general | solution.py:105
  265.4 2.3 copy.247
  267.7 2.5 copy.248
  270.2 2.7 copy.250
  272.9 5.9 %fusion.86 = f32[128,32,16]{1,2,0:T(8,128)} fusion(bf16[16,256,128]{1,0,2:T(8,128)(2,1)} %copy.250, bf16[32,256,128]{0,1,2:T(8,128)(2,1)} %copy.249), kind=kOutput, calls=%fused_computation.154 | convolution fusion | flops 33554432 | bytes 3407872 | tf_op jit(solution)/shard_map/ijh,kjh->kih/dot_general | solution.py:102
  278.8 2.4 copy.251
  281.2 2.6 fusion.18
  286.9 2.1 fusion.22
  289.6 2.4 multiply_reduce_fusion
  296.1 1.9 fusion.68
  302.1 2.0 add_convert_fusion
  305.2 4.2 all-to-all-start.6
  309.5 42.8 %all-gather.11.cloned.1.call-done = bf16[32,256,128]{2,1,0:T(8,128)(2,1)} async-done(((bf16[32,16,128]{2,1,0:T(8,128)(2,1)}), bf16[32,256,128]{2,1,0:T(8,128)(2,1)}) %all-gather.11.cloned.1.call-update) | async-done | bytes 2097168 | tf_op jit(solution)/shard_map/all_gather | solution.py:50
  352.3 4.3 copy.260
  356.6 4.3 all-to-all-start.7
  361.2 2.1 copy.266
  363.3 3.1 copy.263
  366.4 2.1 convolution_bitcast_fusion.2
  371.3 15.3 %copy.267 = bf16[32,256,128]{0,1,2:T(8,128)(2,1)} copy(bf16[32,256,128]{2,1,0:T(8,128)(2,1)} %all-gather.11.cloned.1.call-done) | data formatting | bytes 4194304 | tf_op jit(solution)/shard_map/all_gather | solution.py:50
  386.6 4.9 fusion.85
  392.0 3.7 copy.262
  395.7 4.9 copy.264
  400.6 2.6 fusion.84
  408.7 145.6 %all-reduce.13.cloned.1.call-done = (f32[128,640]{1,0:T(8,128)}, f32[128,128]{1,0:T(8,128)}, f32[128,640]{1,0:T(8,128)}, f32[128,128]{1,0:T(8,128)}) async-done(((f32[128,640]{1,0:T(8,128)}, f32[128,128]{1,0:T(8,128)}, f32[128,640]{1,0:T(8,128)}, f32[128,128]{1,0:T(8,128)}), (f32[128,640]{1,0:T(8,128)}, f32[128,128]{1,0:T(8,128)}, f32[128,640]{1,0:T(8,128)}, ...) | async-done | bytes 786448 | tf_op jit(solution)/shard_map/psum | solution.py:173
  554.3 1.5 broadcast_multiply_fusion.2
  555.8 1.9 broadcast_multiply_fusion
  (155 shorter events, 40.9 us)
Async XLA Ops:
  7.2 90.8 %copy-start = (bf16[128,640]{1,0:T(8,128)(2,1)S(1)}, bf16[128,640]{1,0:T(8,128)(2,1)}, u32[]{:S(2)}) copy-start(bf16[128,640]{1,0:T(8,128)(2,1)} %param.12) | copy-start | bytes 491524
  7.2 65.1 %all-gather.5.cloned.1.call-start = ((), (), s32[]{:S(2)}) async-start(), calls=%async_computation.8 | async-start | bytes 2228224 | tf_op jit(solution)/shard_map/all_gather | solution.py:50
  11.2 0.6 copy-start.15
  14.1 131.7 %all-gather.7.cloned.1.call-start = ((), (), s32[]{:S(2)}) async-start(), calls=%async_computation.9 | async-start | bytes 2228224 | tf_op jit(solution)/shard_map/all_gather | solution.py:50
  93.6 2.2 copy-start.2
  93.6 2.2 copy-start.21
  95.7 1.6 copy-start.17
  97.3 0.6 copy-start.18
  98.4 1.1 copy-start.1
  100.3 1.1 copy-start.4
  101.4 48.6 %all-to-all-start.2 = ((bf16[8,32,16,128]{3,2,1,0:T(8,128)(2,1)}), bf16[8,32,16,128]{3,2,1,0:T(8,128)(2,1)}, u32[]{:S(2)}, u32[]{:S(2)}) async-start(bf16[8,32,16,128]{3,2,1,0:T(8,128)(2,1)} %broadcast_in_dim.25), calls=%async_computation.2 | async-start | bytes 2097152 | tf_op jit(solution)/shard_map/all_to_all | solution.py:16
  150.1 32.6 %all-to-all-start.3 = ((bf16[32,256,128]{2,0,1:T(8,128)(2,1)}), bf16[32,256,128]{2,0,1:T(8,128)(2,1)}, u32[]{:S(2)}, u32[]{:S(2)}) async-start(bf16[32,256,128]{2,0,1:T(8,128)(2,1)} %copy.231), calls=%async_computation.3 | async-start | bytes 4194304 | tf_op jit(solution)/shard_map/all_to_all | solution.py:68
  154.4 86.7 %all-gather.9.cloned.1.call-start = ((), (), s32[]{:S(2)}) async-start(), calls=%async_computation.10 | async-start | bytes 2228224 | tf_op jit(solution)/shard_map/all_gather | solution.py:50
  194.8 1.8 copy-start.20
  196.6 84.6 %copy-start.10 = (f32[32,16]{1,0:T(8,128)}, f32[32,16]{1,0:T(8,128)S(1)}, u32[]{:S(2)}) copy-start(f32[32,16]{1,0:T(8,128)S(1)} %copy.238) | copy-start | bytes 6148
  198.9 82.3 %copy-start.12 = (f32[32,16]{1,0:T(8,128)}, f32[32,16]{1,0:T(8,128)S(1)}, u32[]{:S(2)}) copy-start(f32[32,16]{1,0:T(8,128)S(1)} %copy.240) | copy-start | bytes 6148
  219.8 47.9 %all-to-all-start.5 = ((bf16[256,16,128]{2,1,0:T(8,128)(2,1)}), bf16[256,16,128]{2,1,0:T(8,128)(2,1)}, u32[]{:S(2)}, u32[]{:S(2)}) async-start(bf16[256,16,128]{2,1,0:T(8,128)(2,1)} %bitcast.137), calls=%async_computation.5 | async-start | bytes 2097152 | tf_op jit(solution)/shard_map/all_to_all | solution.py:64
  225.9 126.4 %all-gather.11.cloned.1.call-start = ((), (), s32[]{:S(2)}) async-start(), calls=%async_computation.11 | async-start | bytes 2228224 | tf_op jit(solution)/shard_map/all_gather | solution.py:50
  283.7 1.5 copy-start.22
  283.7 1.5 copy-start.24
  283.7 1.5 copy-start.26
  283.8 1.5 copy-start.28
  283.8 1.5 copy-start.30
  283.8 1.5 copy-start.19
  289.0 0.7 copy-start.5
  289.6 14.5 %copy-start.3 = (bf16[32,16,128]{2,1,0:T(8,128)(2,1)S(1)}, bf16[32,16,128]{2,1,0:T(8,128)(2,1)}, u32[]{:S(2)}) copy-start(bf16[32,16,128]{2,1,0:T(8,128)(2,1)} %get-tuple-element.32) | copy-start | bytes 393220
  305.2 51.4 %all-to-all-start.6 = ((bf16[8,32,16,128]{3,2,1,0:T(8,128)(2,1)}), bf16[8,32,16,128]{3,2,1,0:T(8,128)(2,1)}, u32[]{:S(2)}, u32[]{:S(2)}) async-start(bf16[8,32,16,128]{3,2,1,0:T(8,128)(2,1)} %broadcast_in_dim.62), calls=%async_computation.6 | async-start | bytes 2097152 | tf_op jit(solution)/shard_map/all_to_all | solution.py:16
  356.6 35.4 %all-to-all-start.7 = ((bf16[32,256,128]{2,0,1:T(8,128)(2,1)}), bf16[32,256,128]{2,0,1:T(8,128)(2,1)}, u32[]{:S(2)}, u32[]{:S(2)}) async-start(bf16[32,256,128]{2,0,1:T(8,128)(2,1)} %copy.260), calls=%async_computation.7 | async-start | bytes 4194304 | tf_op jit(solution)/shard_map/all_to_all | solution.py:68
  360.9 193.3 %all-reduce.13.cloned.1.call-start = ((), (), s32[]{:S(2)}) async-start(), calls=%async_computation.12 | async-start | bytes 1572864 | tf_op jit(solution)/shard_map/psum | solution.py:173
  363.3 3.1 copy-start.11
  363.3 3.1 copy-start.13
  363.3 3.1 copy-start.14
  366.4 2.1 copy-start.6
  368.5 1.1 copy-start.23
  368.5 1.1 copy-start.25
  368.5 1.1 copy-start.27
  368.5 1.2 copy-start.29
  368.5 1.2 copy-start.31
  403.7 1.0 copy-start.7
  404.6 1.5 copy-start.8
  404.6 1.5 copy-start.9
  406.1 0.9 copy-start.16
Sparse Core Ops, SparseCore 0:
  14.2 58.0 all-gather.4
  100.5 45.2 all-gather.6
  157.6 47.5 all-gather.8
  304.2 48.0 all-gather.10
  407.7 146.5 all-reduce.12
where the time goes:
time: 566 us; the launch traced here: 564 us
  waiting for transfers between devices  254 us (45%)
  local copies, waits for them, and re-layouts  130 us (23%)
  blocking collectives  71.5 us (13%)
  matrix products  47.2 us (8%)
  starting transfers between devices  23.8 us (4%)
  other arithmetic  23.6 us (4%)
  between operations  14.2 us (3%)
    psum x1, waiting for transfers between devices, local(): lax.psum((out_in_part, out_out_part, in_in_part, in_out_part), ('row', 'c...  146 us
    all_gather x4, waiting for transfers between devices, cols_of(): lax.all_gather(shortened(tiles), 'col', axis=1, tiled=True)  83.4 us
    all_gather x6, local copies, waits for them, and re-layouts, cols_of(): lax.all_gather(shortened(tiles), 'col', axis=1, tiled=True)  69.7 us
    all_to_all x2, blocking collectives, from_everyone(): return lax.all_to_all(copies, axis, split_axis=0, concat_axis=0, tiled=True)  40 us
    all_to_all x1, blocking collectives, to_row_blocks(): return lax.all_to_all(panel, 'col', split_axis=0, concat_axis=1, tiled=True)  31.5 us
    all_to_all x2, waiting for transfers between devices, to_col_blocks(): return lax.all_to_all(panel, 'row', split_axis=1, concat_axis=0, tiled=True)  24.5 us
    all_to_all x4, local copies, waits for them, and re-layouts, to_col_blocks(): return lax.all_to_all(panel, 'row', split_axis=1, concat_axis=0, tiled=True)  17.2 us
  transfers between devices with their start and end apart: 10, of which 5 were waited for; matrix products, arithmetic and copies ran while one was open for 20% of the time, Pallas kernels for 0%

commit v1 on v0

--- a/solution.py
+++ b/solution.py
@@ -61,7 +61,10 @@
 
 
 def to_row_blocks(panel):
-    return lax.all_to_all(panel, "col", split_axis=0, concat_axis=1, tiled=True)
+    return jnp.concatenate(
+        lax.all_to_all(jnp.stack(jnp.split(panel, lax.axis_size("col"), axis=0)), "col", 0, 0),
+        axis=1,
+    )
 
 
 def to_col_blocks(panel):

time: 566 us -> 619 us (1.094); the launches traced: 564 us -> 610 us
  blocking collectives: 71.5 us -> 26.2 us
  waiting for transfers between devices: 254 us -> 297 us
  local copies, waits for them, and re-layouts: 130 us -> 155 us
  starting transfers between devices: 23.8 us -> 45.9 us
    all_to_all x3 -> x1, blocking collectives: 71.5 us -> 26.2 us  [to_row_blocks(): lax.all_to_all(jnp.stack(jnp.split(panel, lax.axis_size('col'), axis=0)),...]
    all_to_all x2 -> x4, waiting for transfers between devices: 0.01 us -> 27.4 us  [from_everyone(): return lax.all_to_all(copies, axis, split_axis=0, concat_axis=0, tiled=True)]
    unnamed x70 -> x100, local copies, waits for them, and re-layouts: 6.82 us -> 28.9 us
    all_gather x4, waiting for transfers between devices: 83.4 us -> 99.4 us  [cols_of(): lax.all_gather(shortened(tiles), 'col', axis=1, tiled=True)]
    all_to_all x2, starting transfers between devices: 8.7 us -> 20.5 us  [to_col_blocks(): return lax.all_to_all(panel, 'row', split_axis=1, concat_axis=0, tiled=True)]
    all_to_all x2 -> x4, starting transfers between devices: 8.48 us -> 18.7 us  [from_everyone(): return lax.all_to_all(copies, axis, split_axis=0, concat_axis=0, tiled=True)]
    all_to_all x4 -> x0, local copies, waits for them, and re-layouts: 9.12 us -> none  [to_row_blocks(): return lax.all_to_all(panel, 'col', split_axis=0, concat_axis=1, tiled=True)]
    reshape x0 -> x4, local copies, waits for them, and re-layouts: none -> 9.1 us  [to_row_blocks(): jnp.concatenate(lax.all_to_all(jnp.stack(jnp.split(panel, lax.axis_size('...]
  transfers between devices with their start and end apart: 10 -> 12, of which waited for: 5 -> 7; matrix products, arithmetic and copies ran while one was open for 20% -> 19% of each run, Pallas kernels for 0% -> 0%
where the time goes in v1:
time: 619 us; the launch traced here: 610 us
  waiting for transfers between devices  297 us (48%)
  local copies, waits for them, and re-layouts  155 us (25%)
  matrix products  47.2 us (8%)
  starting transfers between devices  45.9 us (7%)
  blocking collectives  26.2 us (4%)
  other arithmetic  23.7 us (4%)
  between operations  14.6 us (2%)
    psum x1, waiting for transfers between devices, local(): lax.psum((out_in_part, out_out_part, in_in_part, in_out_part), ('row', 'c...  146 us
    all_gather x4, waiting for transfers between devices, cols_of(): lax.all_gather(shortened(tiles), 'col', axis=1, tiled=True)  99.4 us
    all_gather x6, local copies, waits for them, and re-layouts, cols_of(): lax.all_gather(shortened(tiles), 'col', axis=1, tiled=True)  69.6 us
    unnamed x100, local copies, waits for them, and re-layouts  28.9 us
    all_to_all x4, waiting for transfers between devices, from_everyone(): return lax.all_to_all(copies, axis, split_axis=0, concat_axis=0, tiled=True)  27.4 us
    all_to_all x1, blocking collectives, to_row_blocks(): lax.all_to_all(jnp.stack(jnp.split(panel, lax.axis_size('col'), axis=0)),...  26.2 us
    all_to_all x2, waiting for transfers between devices, to_col_blocks(): return lax.all_to_all(panel, 'row', split_axis=1, concat_axis=0, tiled=True)  23.6 us
    all_to_all x2, starting transfers between devices, to_col_blocks(): return lax.all_to_all(panel, 'row', split_axis=1, concat_axis=0, tiled=True)  20.5 us
  transfers between devices with their start and end apart: 12, of which 7 were waited for; matrix products, arithmetic and copies ran while one was open for 19% of the time, Pallas kernels for 0%

profile of v1, /device:TPU:1, one launch (start us, length us, event | category | flops | bytes accessed | tf_op | source)
XLA Modules:
  0.0 610.4 jit_solution(8245358000467417501)
XLA Ops:
  15.2 5.9 all-to-all-start
  21.9 13.8 %all-to-all-done = bf16[8,32,16,128]{3,2,1,0:T(8,128)(2,1)S(1)} async-done(((bf16[8,32,16,128]{3,2,1,0:T(8,128)(2,1)}), bf16[8,32,16,128]{3,2,1,0:T(8,128)(2,1)S(1)}, u32[]{:S(2)}, u32[]{:S(2)}) %all-to-all-start) | async-done | bytes 1048608 | tf_op jit(solution)/shard_map/all_to_all | solution.py:16
  36.0 26.2 %all_to_all.66 = bf16[16,16,16,128]{3,2,1,0:T(8,128)(2,1)S(1)} all-to-all(bf16[16,16,16,128]{3,2,1,0:T(8,128)(2,1)S(1)} %constant_dynamic-update-slice_fusion), channel_id=1, replica_groups=mesh['row'=8,'col'=16] {'col'}, dimensions={0} | all-to-all | bytes 2097152 | tf_op jit(solution)/shard_map/all_to_all | solution.py:65
  63.4 2.7 copy.219
  66.1 15.1 %all-gather.5.cloned.1.call-done = bf16[32,256,128]{2,1,0:T(8,128)(2,1)} async-done(((bf16[32,16,128]{2,1,0:T(8,128)(2,1)}), bf16[32,256,128]{2,1,0:T(8,128)(2,1)}) %all-gather.5.cloned.1.call-update) | async-done | bytes 2097168 | tf_op jit(solution)/shard_map/all_gather | solution.py:50
  81.2 15.3 %copy.220 = bf16[32,256,128]{0,1,2:T(8,128)(2,1)} copy(bf16[32,256,128]{2,1,0:T(8,128)(2,1)} %all-gather.5.cloned.1.call-done) | data formatting | bytes 4194304 | tf_op jit(solution)/shard_map/all_gather | solution.py:50
  96.5 6.0 bitcast_reduce_fusion.1
  110.4 4.2 all-to-all-start.2
  114.7 41.3 %all-gather.7.cloned.1.call-done = bf16[32,256,128]{2,1,0:T(8,128)(2,1)} async-done(((bf16[32,16,128]{2,1,0:T(8,128)(2,1)}), bf16[32,256,128]{2,1,0:T(8,128)(2,1)}) %all-gather.7.cloned.1.call-update) | async-done | bytes 2097168 | tf_op jit(solution)/shard_map/all_gather | solution.py:50
  156.0 4.3 copy.230
  160.3 16.1 %all-to-all-start.3 = ((bf16[32,256,128]{2,0,1:T(8,128)(2,1)}), bf16[32,256,128]{2,0,1:T(8,128)(2,1)}, u32[]{:S(2)}, u32[]{:S(2)}) async-start(bf16[32,256,128]{2,0,1:T(8,128)(2,1)} %copy.230), calls=%async_computation.3 | async-start | bytes 4194304 | tf_op jit(solution)/shard_map/all_to_all | solution.py:71
  176.4 3.0 copy.233
  179.4 23.6 %all-to-all-done.3 = bf16[32,256,128]{2,0,1:T(8,128)(2,1)} async-done(((bf16[32,256,128]{2,0,1:T(8,128)(2,1)}), bf16[32,256,128]{2,0,1:T(8,128)(2,1)}, u32[]{:S(2)}, u32[]{:S(2)}) %all-to-all-start.3) | async-done | bytes 2097184 | tf_op jit(solution)/shard_map/all_to_all | solution.py:71
  203.0 3.8 copy.232
  206.7 4.9 copy.234
  211.6 3.6 bitcast_reduce_fusion
  217.0 2.0 multiply_reduce_fusion.1
  223.2 4.2 all-to-all-start.4
  228.2 13.6 %all-to-all-done.4 = bf16[8,32,16,128]{3,2,1,0:T(8,128)(2,1)} async-done(((bf16[8,32,16,128]{3,2,1,0:T(8,128)(2,1)}), bf16[8,32,16,128]{3,2,1,0:T(8,128)(2,1)}, u32[]{:S(2)}, u32[]{:S(2)}) %all-to-all-start.4) | async-done | bytes 1048608 | tf_op jit(solution)/shard_map/all_to_all | solution.py:16
  265.2 6.4 %all-to-all-start.5 = ((bf16[16,16,16,128]{3,2,1,0:T(8,128)(2,1)}), bf16[16,16,16,128]{3,2,1,0:T(8,128)(2,1)}, u32[]{:S(2)}, u32[]{:S(2)}) async-start(bf16[16,16,16,128]{3,2,1,0:T(8,128)(2,1)} %constant_dynamic-update-slice_fusion.16), calls=%async_computation.5 | async-start | bytes 2097152 | tf_op jit(solution)/shard_map/all_to_all | solution.py:65
  271.6 15.2 %copy.245 = bf16[32,256,128]{0,1,2:T(8,128)(2,1)} copy(bf16[32,256,128]{2,1,0:T(8,128)(2,1)} %all-gather.7.cloned.1.call-done) | data formatting | bytes 4194304 | tf_op jit(solution)/shard_map/all_gather | solution.py:50
  286.9 15.3 %copy.248 = bf16[32,256,128]{0,1,2:T(8,128)(2,1)} copy(bf16[32,256,128]{2,1,0:T(8,128)(2,1)} %all-gather.9.cloned.1.call-done) | data formatting | bytes 4194304 | tf_op jit(solution)/shard_map/all_gather | solution.py:50
  302.2 3.0 copy.244
  305.2 5.9 fusion.83
  311.0 2.4 copy.246
  313.4 2.5 copy.247
  315.9 2.7 copy.249
  318.6 5.9 fusion.86
  324.5 2.4 copy.250
  326.9 2.6 fusion.18
  332.6 2.1 fusion.22
  335.3 2.4 multiply_reduce_fusion
  341.8 1.9 fusion.68
  347.8 2.0 add_convert_fusion
  350.9 4.2 all-to-all-start.6
  355.2 42.9 %all-gather.11.cloned.1.call-done = bf16[32,256,128]{2,1,0:T(8,128)(2,1)} async-done(((bf16[32,16,128]{2,1,0:T(8,128)(2,1)}), bf16[32,256,128]{2,1,0:T(8,128)(2,1)}) %all-gather.11.cloned.1.call-update) | async-done | bytes 2097168 | tf_op jit(solution)/shard_map/all_gather | solution.py:50
  398.0 4.2 copy.259
  402.3 4.4 all-to-all-start.7
  406.9 2.1 copy.265
  409.0 3.1 copy.262
  412.1 2.1 convolution_bitcast_fusion.2
  416.9 15.3 %copy.266 = bf16[32,256,128]{0,1,2:T(8,128)(2,1)} copy(bf16[32,256,128]{2,1,0:T(8,128)(2,1)} %all-gather.11.cloned.1.call-done) | data formatting | bytes 4194304 | tf_op jit(solution)/shard_map/all_gather | solution.py:50
  432.2 4.9 fusion.85
  437.6 3.7 copy.261
  441.4 4.9 copy.263
  446.3 2.6 fusion.84
  454.3 145.7 %all-reduce.13.cloned.1.call-done = (f32[128,640]{1,0:T(8,128)}, f32[128,128]{1,0:T(8,128)}, f32[128,640]{1,0:T(8,128)}, f32[128,128]{1,0:T(8,128)}) async-done(((f32[128,640]{1,0:T(8,128)}, f32[128,128]{1,0:T(8,128)}, f32[128,640]{1,0:T(8,128)}, f32[128,128]{1,0:T(8,128)}), (f32[128,640]{1,0:T(8,128)}, f32[128,128]{1,0:T(8,128)}, f32[128,640]{1,0:T(8,128)}, ...) | async-done | bytes 786448 | tf_op jit(solution)/shard_map/psum | solution.py:176
  601.5 1.9 broadcast_multiply_fusion
  (189 shorter events, 71.5 us)
Async XLA Ops:
  7.2 99.8 %copy-start = (bf16[128,640]{1,0:T(8,128)(2,1)S(1)}, bf16[128,640]{1,0:T(8,128)(2,1)}, u32[]{:S(2)}) copy-start(bf16[128,640]{1,0:T(8,128)(2,1)} %param.12) | copy-start | bytes 491524
  11.2 0.6 copy-start.15
  15.2 20.5 %all-to-all-start = ((bf16[8,32,16,128]{3,2,1,0:T(8,128)(2,1)}), bf16[8,32,16,128]{3,2,1,0:T(8,128)(2,1)S(1)}, u32[]{:S(2)}, u32[]{:S(2)}) async-start(bf16[8,32,16,128]{3,2,1,0:T(8,128)(2,1)} %broadcast_in_dim.24), calls=%async_computation | async-start | bytes 2097152 | tf_op jit(solution)/shard_map/all_to_all | solution.py:16
  21.1 60.1 %all-gather.5.cloned.1.call-start = ((), (), s32[]{:S(2)}) async-start(), calls=%async_computation.8 | async-start | bytes 2228224 | tf_op jit(solution)/shard_map/all_gather | solution.py:50
  21.9 134.1 %all-gather.7.cloned.1.call-start = ((), (), s32[]{:S(2)}) async-start(), calls=%async_computation.9 | async-start | bytes 2228224 | tf_op jit(solution)/shard_map/all_gather | solution.py:50
  102.5 2.2 copy-start.2
  102.5 2.2 copy-start.21
  104.6 1.6 copy-start.17
  106.2 0.6 copy-start.18
  107.3 1.1 copy-start.1
  109.3 1.1 copy-start.4
  110.4 49.9 %all-to-all-start.2 = ((bf16[8,32,16,128]{3,2,1,0:T(8,128)(2,1)}), bf16[8,32,16,128]{3,2,1,0:T(8,128)(2,1)}, u32[]{:S(2)}, u32[]{:S(2)}) async-start(bf16[8,32,16,128]{3,2,1,0:T(8,128)(2,1)} %broadcast_in_dim.25), calls=%async_computation.2 | async-start | bytes 2097152 | tf_op jit(solution)/shard_map/all_to_all | solution.py:16
  160.3 42.7 %all-to-all-start.3 = ((bf16[32,256,128]{2,0,1:T(8,128)(2,1)}), bf16[32,256,128]{2,0,1:T(8,128)(2,1)}, u32[]{:S(2)}, u32[]{:S(2)}) async-start(bf16[32,256,128]{2,0,1:T(8,128)(2,1)} %copy.230), calls=%async_computation.3 | async-start | bytes 4194304 | tf_op jit(solution)/shard_map/all_to_all | solution.py:71
  215.2 1.8 copy-start.20
  217.0 109.9 %copy-start.10 = (f32[32,16]{1,0:T(8,128)}, f32[32,16]{1,0:T(8,128)S(1)}, u32[]{:S(2)}) copy-start(f32[32,16]{1,0:T(8,128)S(1)} %copy.237) | copy-start | bytes 6148
  219.3 107.6 %copy-start.12 = (f32[32,16]{1,0:T(8,128)}, f32[32,16]{1,0:T(8,128)S(1)}, u32[]{:S(2)}) copy-start(f32[32,16]{1,0:T(8,128)S(1)} %copy.239) | copy-start | bytes 6148
  223.2 18.6 %all-to-all-start.4 = ((bf16[8,32,16,128]{3,2,1,0:T(8,128)(2,1)}), bf16[8,32,16,128]{3,2,1,0:T(8,128)(2,1)}, u32[]{:S(2)}, u32[]{:S(2)}) async-start(bf16[8,32,16,128]{3,2,1,0:T(8,128)(2,1)} %broadcast_in_dim.28), calls=%async_computation.4 | async-start | bytes 2097152 | tf_op jit(solution)/shard_map/all_to_all | solution.py:16
  227.5 59.4 %all-gather.9.cloned.1.call-start = ((), (), s32[]{:S(2)}) async-start(), calls=%async_computation.10 | async-start | bytes 2228224 | tf_op jit(solution)/shard_map/all_gather | solution.py:50
  265.2 48.2 %all-to-all-start.5 = ((bf16[16,16,16,128]{3,2,1,0:T(8,128)(2,1)}), bf16[16,16,16,128]{3,2,1,0:T(8,128)(2,1)}, u32[]{:S(2)}, u32[]{:S(2)}) async-start(bf16[16,16,16,128]{3,2,1,0:T(8,128)(2,1)} %constant_dynamic-update-slice_fusion.16), calls=%async_computation.5 | async-start | bytes 2097152 | tf_op jit(solution)/shard_map/all_to_all | solution.py:65
  271.6 126.4 %all-gather.11.cloned.1.call-start = ((), (), s32[]{:S(2)}) async-start(), calls=%async_computation.11 | async-start | bytes 2228224 | tf_op jit(solution)/shard_map/all_gather | solution.py:50
  329.4 1.5 copy-start.22
  329.4 1.5 copy-start.24
  329.4 1.5 copy-start.26
  329.4 1.5 copy-start.28
  329.4 1.5 copy-start.30
  329.5 1.5 copy-start.19
  334.7 0.7 copy-start.5
  335.3 14.5 %copy-start.3 = (bf16[32,16,128]{2,1,0:T(8,128)(2,1)S(1)}, bf16[32,16,128]{2,1,0:T(8,128)(2,1)}, u32[]{:S(2)}) copy-start(bf16[32,16,128]{2,1,0:T(8,128)(2,1)} %get-tuple-element.32) | copy-start | bytes 393220
  350.9 51.4 %all-to-all-start.6 = ((bf16[8,32,16,128]{3,2,1,0:T(8,128)(2,1)}), bf16[8,32,16,128]{3,2,1,0:T(8,128)(2,1)}, u32[]{:S(2)}, u32[]{:S(2)}) async-start(bf16[8,32,16,128]{3,2,1,0:T(8,128)(2,1)} %broadcast_in_dim.62), calls=%async_computation.6 | async-start | bytes 2097152 | tf_op jit(solution)/shard_map/all_to_all | solution.py:16
  402.3 35.3 %all-to-all-start.7 = ((bf16[32,256,128]{2,0,1:T(8,128)(2,1)}), bf16[32,256,128]{2,0,1:T(8,128)(2,1)}, u32[]{:S(2)}, u32[]{:S(2)}) async-start(bf16[32,256,128]{2,0,1:T(8,128)(2,1)} %copy.259), calls=%async_computation.7 | async-start | bytes 4194304 | tf_op jit(solution)/shard_map/all_to_all | solution.py:71
  406.7 193.3 %all-reduce.13.cloned.1.call-start = ((), (), s32[]{:S(2)}) async-start(), calls=%async_computation.12 | async-start | bytes 1572864 | tf_op jit(solution)/shard_map/psum | solution.py:176
  409.0 3.1 copy-start.11
  409.0 3.1 copy-start.13
  409.0 3.1 copy-start.14
  412.1 2.1 copy-start.6
  414.2 1.1 copy-start.23
  414.2 1.1 copy-start.25
  414.2 1.1 copy-start.27
  414.2 1.2 copy-start.29
  414.2 1.2 copy-start.31
  449.3 1.0 copy-start.7
  450.3 1.5 copy-start.8
  450.3 1.5 copy-start.9
  451.8 0.9 copy-start.16
Sparse Core Ops, SparseCore 0:
  24.8 56.3 all-gather.4
  109.4 46.5 all-gather.6
  230.7 46.6 all-gather.8
  349.9 48.0 all-gather.10
  453.4 146.5 all-reduce.12
